TPU v7x, 32 devices: a whole 2x2x4 slice. The times are simulated.
32 devices in a mesh: dp: 8 (over z, y), tensor: 4 (over x, core).
Axes of the slice: x: 2, y: 2, z: 4, core: 2. Of those that a mesh axis runs over, the one named last changes fastest.
Arguments:
- tokens: bfloat16 [8192, 768], P('dp'), may hold values from -6 to 6
- cotangent: bfloat16 [8192, 768], P('dp'), may hold values from -6 to 6
- item_count: int32 [8], P('dp'), may hold values from 0 to 1, as said below
- timestep: int32 [8], P('dp'), may hold values from 0 to 999
- class_id: int32 [8], P('dp'), may hold values from 0 to 1000
- class_table: bfloat16 [1001, 768], replicated, may hold values from -6 to 6
- w_mod: bfloat16 [4608, 768], replicated, may hold values from -0.21875 to 0.21875
- b_mod: bfloat16 [4608], replicated, may hold values from -3 to 3
- k_att: bfloat16 [9, 768], replicated, may hold values from -2 to 2
- w_qkv: bfloat16 [768, 3, 768], P(None, None, 'tensor'), may hold values from -0.21875 to 0.21875
- w_out: bfloat16 [768, 768], P(None, 'tensor'), may hold values from -0.875 to 0.875
- b_out: bfloat16 [768], replicated, may hold values from -2 to 2
- w_up: bfloat16 [768, 3072], P(None, 'tensor'), may hold values from -0.21875 to 0.21875
- b_up: bfloat16 [3072], P('tensor'), may hold values from -2 to 2
- k_ffn: bfloat16 [9, 3072], P(None, 'tensor'), may hold values from -2 to 2
- w_down: bfloat16 [768, 3072], P(None, 'tensor'), may hold values from -0.109375 to 0.109375
- b_down: bfloat16 [768], replicated, may hold values from -2 to 2
Outputs:
- block_out: bfloat16 [8192, 768], P(('dp', 'tensor'))
- grad_tokens: float32 [8192, 768], P(('dp', 'tensor'))
- grad_class_table: float32 [1001, 768], replicated
- grad_w_mod: float32 [4608, 768], P('dp')
- grad_b_mod: float32 [4608], replicated
- grad_k_att: float32 [9, 768], replicated
- grad_w_qkv: float32 [768, 3, 768], P('dp', None, 'tensor')
- grad_w_out: float32 [768, 768], P('dp', 'tensor')
- grad_b_out: float32 [768], replicated
- grad_w_up: float32 [768, 3072], P('dp', 'tensor')
- grad_b_up: float32 [3072], P('tensor')
- grad_k_ffn: float32 [9, 3072], P(None, 'tensor')
- grad_w_down: float32 [768, 3072], P('dp', 'tensor')
- grad_b_down: float32 [768], replicated
Inputs may be any that keep to these rules, and one draw needn't show every extreme that they name: Item slots below item_count of their dp index hold live items, the others padding; some index of dp has all 1 slots live and some none.
All inputs are finite; a program needn't handle non-finite values.
Results may differ from a plain program's by a relative error of at most 0.028.
The roundings to bfloat16 on the way count: a program that leaves them out, or rounds other values in their place, can miss the bound.
Values may be sent and summed in bfloat16 or wider, within the bound.
No kernel may reach another device: no remote copies, remote signals or barrier semaphores. Data moves between devices by JAX's collectives and lax.ppermute only.
A program may use at most 192 MiB of HBM per device.

v0:
```python
import math
import jax
import jax.numpy as jnp
from jax import lax
from jax.sharding import PartitionSpec as P

HEAD_DIM = 64
SIDE = 32
norm_eps = 1e-06
score_scale = 0.125
highest = lax.Precision.HIGHEST


def layer_norm(values):
    center = values - jnp.mean(values, axis=-1, keepdims=True)
    return center * lax.rsqrt(jnp.mean(center * center, axis=-1, keepdims=True) + norm_eps)


def time_features(timestep, width):
    half_width = width // 2
    freqs = jnp.exp(-math.log(10000.0) * jnp.arange(half_width, dtype=jnp.float32) / half_width)
    angles = timestep.astype(jnp.float32)[:, None] * freqs[None, :]
    return jnp.concatenate([jnp.cos(angles), jnp.sin(angles)], axis=1)


def depthwise(field, kernel):
    grid_side = field.shape[1]
    padded = jnp.pad(field, ((0, 0), (1, 1), (1, 1), (0, 0)))
    total = jnp.zeros_like(field)
    for vertical in range(3):
        for horizontal in range(3):
            total = (
                total
                + kernel[vertical * 3 + horizontal]
                * padded[:, vertical : vertical + grid_side, horizontal : horizontal + grid_side]
            )
    return total


def depthwise_back(field, grad_field, kernel):
    grid_side = field.shape[1]
    padded_in = jnp.pad(field, ((0, 0), (1, 1), (1, 1), (0, 0)))
    padded_grad = jnp.pad(grad_field, ((0, 0), (1, 1), (1, 1), (0, 0)))
    input_grad = jnp.zeros_like(field)
    kernel_rows = []
    for vertical in range(3):
        for horizontal in range(3):
            input_grad = (
                input_grad
                + kernel[vertical * 3 + horizontal]
                * padded_grad[
                    :,
                    2 - vertical : 2 - vertical + grid_side,
                    2 - horizontal : 2 - horizontal + grid_side,
                ]
            )
            kernel_rows.append(
                jnp.sum(
                    grad_field
                    * padded_in[
                        :, vertical : vertical + grid_side, horizontal : horizontal + grid_side
                    ],
                    axis=(0, 1, 2),
                )
            )
    return (input_grad, jnp.stack(kernel_rows))


def to_groups(values, items_here):
    half_side = SIDE // 2
    trailing = values.shape[1:]
    shaped = values.reshape((items_here, half_side, 2, half_side, 2) + trailing)
    axes_order = (0, 2, 4, 1, 3) + tuple(range(5, 5 + len(trailing)))
    return shaped.transpose(axes_order).reshape((items_here * 4, half_side * half_side) + trailing)


def from_groups(values, items_here):
    half_side = SIDE // 2
    trailing = values.shape[2:]
    shaped = values.reshape((items_here, 2, 2, half_side, half_side) + trailing)
    axes_order = (0, 3, 1, 4, 2) + tuple(range(5, 5 + len(trailing)))
    return shaped.transpose(axes_order).reshape((items_here * SIDE * SIDE,) + trailing)


def split_project(project, items_here):
    grouped = to_groups(project.reshape(project.shape[0], 3, -1, HEAD_DIM), items_here)
    return (grouped[:, :, 0], grouped[:, :, 1], grouped[:, :, 2])


def attend(project, items_here):
    query, keys, vals = split_project(project, items_here)
    scores = (
        jnp.einsum("bqhd,bkhd->bhqk", query, keys, preferred_element_type=jnp.float32) * score_scale
    )
    top_score = jnp.max(scores, axis=-1, keepdims=True)
    log_total = top_score + jnp.log(jnp.sum(jnp.exp(scores - top_score), axis=-1, keepdims=True))
    probs_low = jnp.exp(scores - log_total).astype(jnp.bfloat16)
    attended = jnp.einsum("bhqk,bkhd->bqhd", probs_low, vals, preferred_element_type=jnp.float32)
    merged = from_groups(attended, items_here)
    return (merged.reshape(merged.shape[0], -1).astype(jnp.bfloat16), log_total)


def attend_back(project, log_total, grad_attended, items_here):
    query, keys, vals = split_project(project, items_here)
    grad_grouped = to_groups(
        grad_attended.reshape(grad_attended.shape[0], -1, HEAD_DIM), items_here
    )
    scores = (
        jnp.einsum("bqhd,bkhd->bhqk", query, keys, preferred_element_type=jnp.float32) * score_scale
    )
    probs = jnp.exp(scores - log_total)
    probs_low = probs.astype(jnp.bfloat16)
    grad_probs = jnp.einsum(
        "bqhd,bkhd->bhqk", grad_grouped, vals, preferred_element_type=jnp.float32
    )
    grad_scores = (
        probs * (grad_probs - jnp.sum(probs * grad_probs, axis=-1, keepdims=True))
    ).astype(jnp.bfloat16)
    grad_query = (
        jnp.einsum("bhqk,bkhd->bqhd", grad_scores, keys, preferred_element_type=jnp.float32)
        * score_scale
    )
    grad_keys = (
        jnp.einsum("bhqk,bqhd->bkhd", grad_scores, query, preferred_element_type=jnp.float32)
        * score_scale
    )
    grad_vals = jnp.einsum(
        "bhqk,bqhd->bkhd", probs_low, grad_grouped, preferred_element_type=jnp.float32
    )
    stacked = jnp.stack([grad_query, grad_keys, grad_vals], axis=2).astype(jnp.bfloat16)
    merged = from_groups(stacked, items_here)
    return merged.reshape(merged.shape[0], 3, -1)


def contract_last(left, right):
    return lax.dot_general(
        left, right, (((1,), (1,)), ((), ())), preferred_element_type=jnp.float32
    )


def contract_first(left, right):
    return lax.dot_general(
        left, right, (((0,), (0,)), ((), ())), preferred_element_type=jnp.float32
    )


def spread_rows(row_hot, table):
    return jnp.dot(row_hot, table, precision=highest, preferred_element_type=jnp.float32)


def item_sums(row_hot, values):
    return lax.dot_general(
        row_hot,
        values,
        (((0,), (0,)), ((), ())),
        precision=highest,
        preferred_element_type=jnp.float32,
    )


def shards(
    tokens,
    cotangent,
    item_count,
    timestep,
    class_id,
    class_table,
    w_mod,
    b_mod,
    k_att,
    w_qkv,
    w_out,
    b_out,
    w_up,
    b_up,
    k_ffn,
    w_down,
    b_down,
):
    items_here = timestep.shape[0]
    total_rows = tokens.shape[0]
    width = tokens.shape[1]
    item_rows = total_rows // items_here
    share_rows = total_rows // lax.axis_size("tensor")
    share_start = lax.axis_index("tensor") * share_rows
    live = (jnp.arange(items_here) < item_count[0]).astype(jnp.float32)
    row_item = (share_start + jnp.arange(share_rows)) // item_rows
    row_hot = (row_item[:, None] == jnp.arange(items_here)[None, :]).astype(jnp.float32)
    live_rows = spread_rows(row_hot, live[:, None])
    k_att_f = k_att.astype(jnp.float32)
    k_ffn_f = k_ffn.astype(jnp.float32)
    one_hot = class_id[:, None] == jnp.arange(class_table.shape[0])[None, :]
    cond = time_features(timestep, width) + jnp.dot(
        one_hot.astype(jnp.bfloat16), class_table, preferred_element_type=jnp.float32
    )
    act_low = jax.nn.silu(cond).astype(jnp.bfloat16)
    modulate = contract_last(act_low, w_mod) + b_mod.astype(jnp.float32)
    pieces = jnp.split(modulate, 6, axis=1)
    shift_att = pieces[0][:, None, :]
    scale_att = pieces[1][:, None, :]
    scale_att_rows = spread_rows(row_hot, pieces[1])
    gate_att_rows = spread_rows(row_hot, pieces[2])
    shift_ffn_rows = spread_rows(row_hot, pieces[3])
    scale_ffn_rows = spread_rows(row_hot, pieces[4])
    gate_ffn_rows = spread_rows(row_hot, pieces[5])
    x_flat = tokens.astype(jnp.float32)
    x_items = x_flat.reshape(items_here, item_rows, width)

    def forward_pass(source):
        normed = layer_norm(source)
        shaped = normed * (1.0 + scale_att) + shift_att
        mixed = (
            depthwise(shaped.reshape(items_here, SIDE, SIDE, width), k_att_f)
            .reshape(total_rows, width)
            .astype(jnp.bfloat16)
        )
        project = jnp.einsum(
            "td,dcj->tcj", mixed, w_qkv, preferred_element_type=jnp.float32
        ).astype(jnp.bfloat16)
        attended, log_total = attend(project, items_here)
        branch = lax.psum_scatter(
            contract_last(attended, w_out).astype(jnp.bfloat16),
            "tensor",
            scatter_dimension=0,
            tiled=True,
        ).astype(jnp.float32) + b_out.astype(jnp.float32)
        source_share = lax.dynamic_slice_in_dim(
            source.reshape(total_rows, width), share_start, share_rows, 0
        )
        middle = source_share + gate_att_rows * branch
        normed_ffn = layer_norm(middle)
        shaped_share = (normed_ffn * (1.0 + scale_ffn_rows) + shift_ffn_rows).astype(jnp.bfloat16)
        shaped_ffn = lax.all_gather(shaped_share, "tensor", axis=0, tiled=True)
        hidden = jnp.dot(shaped_ffn, w_up, preferred_element_type=jnp.float32) + b_up.astype(
            jnp.float32
        )
        convolved = depthwise(hidden.reshape(items_here, SIDE, SIDE, -1), k_ffn_f).reshape(
            total_rows, -1
        )
        activated = jax.nn.gelu(convolved).astype(jnp.bfloat16)
        branch_ffn = lax.psum_scatter(
            contract_last(activated, w_down).astype(jnp.bfloat16),
            "tensor",
            scatter_dimension=0,
            tiled=True,
        ).astype(jnp.float32) + b_down.astype(jnp.float32)
        result = middle + gate_ffn_rows * branch_ffn
        return (
            normed,
            shaped,
            mixed,
            project,
            attended,
            log_total,
            branch,
            middle,
            normed_ffn,
            shaped_ffn,
            hidden,
            convolved,
            activated,
            branch_ffn,
            result,
        )

    saved = forward_pass(x_items)
    block_out = (saved[14] * live_rows).astype(jnp.bfloat16)
    again = lax.optimization_barrier((x_items, block_out))[0]
    saved = forward_pass(again)
    (
        normed,
        shaped,
        mixed,
        project,
        attended,
        log_total,
        branch,
        middle,
        normed_ffn,
        shaped_ffn,
        hidden,
        convolved,
        activated,
        branch_ffn,
        result,
    ) = saved
    cot_share = lax.dynamic_slice_in_dim(cotangent, share_start, share_rows, 0)
    grad_out = cot_share.astype(jnp.float32) * live_rows
    grad_gate_ffn = item_sums(row_hot, grad_out * branch_ffn)
    grad_branch_share = (grad_out * gate_ffn_rows).astype(jnp.bfloat16)
    grad_branch_ffn = lax.all_gather(grad_branch_share, "tensor", axis=0, tiled=True)
    grad_b_down = jnp.sum(grad_branch_ffn.astype(jnp.float32), axis=0)
    grad_w_down = contract_first(grad_branch_ffn, activated)
    grad_activated = jnp.dot(grad_branch_ffn, w_down, preferred_element_type=jnp.float32)
    gelu_value, gelu_back = jax.vjp(jax.nn.gelu, convolved)
    grad_convolved = gelu_back(grad_activated)[0]
    grad_hidden, grad_k_ffn = depthwise_back(
        hidden.reshape(items_here, SIDE, SIDE, -1),
        grad_convolved.reshape(items_here, SIDE, SIDE, -1),
        k_ffn_f,
    )
    grad_hidden = grad_hidden.reshape(total_rows, -1).astype(jnp.bfloat16)
    grad_b_up = jnp.sum(grad_hidden.astype(jnp.float32), axis=0)
    grad_w_up = contract_first(shaped_ffn, grad_hidden)
    grad_shaped_ffn = lax.psum_scatter(
        contract_last(grad_hidden, w_up).astype(jnp.bfloat16),
        "tensor",
        scatter_dimension=0,
        tiled=True,
    ).astype(jnp.float32)
    grad_scale_ffn = item_sums(row_hot, grad_shaped_ffn * normed_ffn)
    grad_shift_ffn = item_sums(row_hot, grad_shaped_ffn)
    norm_value, norm_back_ffn = jax.vjp(layer_norm, middle)
    grad_middle = grad_out + norm_back_ffn(grad_shaped_ffn * (1.0 + scale_ffn_rows))[0]
    grad_gate_att = item_sums(row_hot, grad_middle * branch)
    grad_attn_share = (grad_middle * gate_att_rows).astype(jnp.bfloat16)
    grad_branch = lax.all_gather(grad_attn_share, "tensor", axis=0, tiled=True)
    grad_b_out = jnp.sum(grad_branch.astype(jnp.float32), axis=0)
    grad_w_out = contract_first(grad_branch, attended)
    grad_attended = jnp.dot(grad_branch, w_out, preferred_element_type=jnp.float32).astype(
        jnp.bfloat16
    )
    grad_project = attend_back(project, log_total, grad_attended, items_here)
    grad_w_qkv = jnp.einsum("td,tcj->dcj", mixed, grad_project, preferred_element_type=jnp.float32)
    grad_mixed_share = lax.psum_scatter(
        jnp.einsum("tcj,dcj->td", grad_project, w_qkv, preferred_element_type=jnp.float32).astype(
            jnp.bfloat16
        ),
        "tensor",
        scatter_dimension=0,
        tiled=True,
    )
    grad_mixed = lax.all_gather(grad_mixed_share, "tensor", axis=0, tiled=True).astype(jnp.float32)
    grad_shaped, grad_k_att = depthwise_back(
        shaped.reshape(items_here, SIDE, SIDE, width),
        grad_mixed.reshape(items_here, SIDE, SIDE, width),
        k_att_f,
    )
    grad_shaped_share = lax.dynamic_slice_in_dim(
        grad_shaped.reshape(total_rows, width), share_start, share_rows, 0
    )
    normed_share = lax.dynamic_slice_in_dim(
        normed.reshape(total_rows, width), share_start, share_rows, 0
    )
    grad_scale_att = item_sums(row_hot, grad_shaped_share * normed_share)
    grad_shift_att = item_sums(row_hot, grad_shaped_share)
    x_share = lax.dynamic_slice_in_dim(x_flat, share_start, share_rows, 0)
    norm_first, norm_back_att = jax.vjp(layer_norm, x_share)
    grad_tokens = grad_middle + norm_back_att(grad_shaped_share * (1.0 + scale_att_rows))[0]
    mod_partial = jnp.concatenate(
        [
            grad_shift_att,
            grad_scale_att,
            grad_gate_att,
            grad_shift_ffn,
            grad_scale_ffn,
            grad_gate_ffn,
        ],
        axis=1,
    )
    grad_modulate = lax.psum(mod_partial, "tensor").astype(jnp.bfloat16)
    grad_b_mod = jnp.sum(grad_modulate.astype(jnp.float32), axis=0)
    grad_w_mod = contract_first(grad_modulate, act_low)
    grad_act = jnp.dot(grad_modulate, w_mod, preferred_element_type=jnp.float32)
    silu_value, silu_back = jax.vjp(jax.nn.silu, cond)
    grad_cond = silu_back(grad_act)[0]
    grad_class = lax.dot_general(
        one_hot.astype(jnp.float32),
        grad_cond,
        (((0,), (0,)), ((), ())),
        precision=highest,
        preferred_element_type=jnp.float32,
    )
    summed_qkv, summed_out, summed_up, summed_down, summed_mod = (
        lax.psum_scatter(grad_w_qkv, "dp", scatter_dimension=0, tiled=True),
        lax.psum_scatter(grad_w_out, "dp", scatter_dimension=0, tiled=True),
        lax.psum_scatter(grad_w_up, "dp", scatter_dimension=0, tiled=True),
        lax.psum_scatter(grad_w_down, "dp", scatter_dimension=0, tiled=True),
        lax.psum_scatter(grad_w_mod, "dp", scatter_dimension=0, tiled=True),
    )
    small_sums = lax.psum(
        (grad_k_att, grad_k_ffn, grad_b_up, grad_b_out, grad_b_down, grad_b_mod, grad_class), "dp"
    )
    (
        summed_k_att,
        summed_k_ffn,
        summed_b_up,
        summed_b_out,
        summed_b_down,
        summed_b_mod,
        summed_class,
    ) = small_sums
    return (
        block_out,
        grad_tokens,
        summed_class,
        summed_mod,
        summed_b_mod,
        summed_k_att,
        summed_qkv,
        summed_out,
        summed_b_out,
        summed_up,
        summed_b_up,
        summed_k_ffn,
        summed_down,
        summed_b_down,
    )


def solution(mesh):
    placed = (
        P("dp", None),
        P("dp", None),
        P("dp"),
        P("dp"),
        P("dp"),
        P(),
        P(),
        P(),
        P(),
        P(None, None, "tensor"),
        P(None, "tensor"),
        P(),
        P(None, "tensor"),
        P("tensor"),
        P(None, "tensor"),
        P(None, "tensor"),
        P(),
    )
    return jax.shard_map(
        shards,
        mesh=mesh,
        in_specs=placed,
        out_specs=(
            P(("dp", "tensor"), None),
            P(("dp", "tensor"), None),
            P(),
            P("dp", None),
            P(),
            P(),
            P("dp", None, "tensor"),
            P("dp", "tensor"),
            P(),
            P("dp", "tensor"),
            P("tensor"),
            P(None, "tensor"),
            P("dp", "tensor"),
            P(),
        ),
        check_vma=False,
    )
```

profile of v0, /device:TPU:0, one launch (start us, length us, event | category | flops | bytes accessed | tf_op | source)
XLA Modules:
  0.0 1077.7 jit_solution(4446822066755356792)
XLA Ops:
  13.5 5.1 convolution_reduce_fusion
  20.1 4.5 fusion.23
  27.6 5.4 reshape_reshape.15
  39.4 3.5 convert_bitcast_fusion
  42.9 27.1 %reduce-scatter.12.cloned.1.call-done = bf16[256,768]{1,0:T(8,128)(2,1)} async-done(((bf16[1024,768]{1,0:T(8,128)(2,1)}), bf16[256,768]{1,0:T(8,128)(2,1)}) %reduce-scatter.12.cloned.1.call-update) | async-done | bytes 393232 | tf_op jit(solution)/shard_map/reduce_scatter | solution.py:221
  76.5 19.5 %all-gather.6.cloned.1.call-done = bf16[1024,768]{1,0:T(8,128)(2,1)} async-done(((bf16[256,768]{1,0:T(8,128)(2,1)}), bf16[1024,768]{1,0:T(8,128)(2,1)}) %all-gather.6.cloned.1.call-update) | async-done | bytes 1572880 | tf_op jit(solution)/shard_map/all_gather | solution.py:233
  96.0 3.2 convolution_add_fusion.1
  99.3 4.4 fusion.39
  110.6 25.3 %reduce-scatter.14.cloned.1.call-done = bf16[256,768]{1,0:T(8,128)(2,1)} async-done(((bf16[1024,768]{1,0:T(8,128)(2,1)}), bf16[256,768]{1,0:T(8,128)(2,1)}) %reduce-scatter.14.cloned.1.call-update) | async-done | bytes 393232 | tf_op jit(solution)/shard_map/reduce_scatter | solution.py:241
  135.9 2.7 fusion.99
  141.8 4.5 add_convert_fusion
  149.2 5.4 reshape_reshape.16
  158.6 2.8 copy.57
  161.4 3.2 convert_element_type.230
  164.6 2.7 convolution_convert_fusion.2
  167.4 28.3 %reduce-scatter.16.cloned.1.call-done = bf16[256,768]{1,0:T(8,128)(2,1)} async-done(((bf16[1024,768]{1,0:T(8,128)(2,1)}), bf16[256,768]{1,0:T(8,128)(2,1)}) %reduce-scatter.16.cloned.1.call-update) | async-done | bytes 393232 | tf_op jit(solution)/shard_map/reduce_scatter | solution.py:221
  200.1 18.9 %all-gather.10.cloned.1.call-done = bf16[1024,768]{1,0:T(8,128)(2,1)} async-done(((bf16[256,768]{1,0:T(8,128)(2,1)}), bf16[1024,768]{1,0:T(8,128)(2,1)}) %all-gather.10.cloned.1.call-update) | async-done | bytes 1572880 | tf_op jit(solution)/shard_map/all_gather | solution.py:233
  219.0 3.2 convolution_add_fusion
  223.9 5.7 multiply_add_fusion
  229.6 10.6 all-gather.8.cloned.1.call-done
  240.2 8.5 multiply_reduce_fusion.4
  250.4 5.1 convert_reduce_fusion.1
  259.3 28.3 %reduce-scatter.18.cloned.1.call-done = bf16[256,768]{1,0:T(8,128)(2,1)} async-done(((bf16[1024,768]{1,0:T(8,128)(2,1)}), bf16[256,768]{1,0:T(8,128)(2,1)}) %reduce-scatter.18.cloned.1.call-update) | async-done | bytes 393232 | tf_op jit(solution)/shard_map/reduce_scatter | solution.py:305
  294.1 19.6 %all-gather.12.cloned.1.call-done = bf16[1024,768]{1,0:T(8,128)(2,1)} async-done(((bf16[256,768]{1,0:T(8,128)(2,1)}), bf16[1024,768]{1,0:T(8,128)(2,1)}) %all-gather.12.cloned.1.call-update) | async-done | bytes 1572880 | tf_op jit(solution)/shard_map/all_gather | solution.py:317
  313.7 2.8 convolution_convert_fusion.6
  318.5 3.2 reshape_reshape.17
  328.3 3.2 copy.68
  331.6 3.4 reshape_reshape.18
  335.0 4.4 bitcast_convert_fusion
  339.5 28.3 %reduce-scatter.20.cloned.1.call-done = bf16[256,768]{1,0:T(8,128)(2,1)} async-done(((bf16[1024,768]{1,0:T(8,128)(2,1)}), bf16[256,768]{1,0:T(8,128)(2,1)}) %reduce-scatter.20.cloned.1.call-update) | async-done | bytes 393232 | tf_op jit(solution)/shard_map/reduce_scatter | solution.py:325
  370.9 4.7 fusion.154
  375.7 4.4 fusion.155
  380.2 2.9 fusion.153
  383.2 4.7 fusion.152
  390.9 4.4 fusion.72
  400.9 18.9 %reduce-scatter.22.cloned.1.call-done = bf16[256,768]{1,0:T(8,128)(2,1)} async-done(((bf16[1024,768]{1,0:T(8,128)(2,1)}), bf16[256,768]{1,0:T(8,128)(2,1)}) %reduce-scatter.22.cloned.1.call-update) | async-done | bytes 393232 | tf_op jit(solution)/shard_map/reduce_scatter | solution.py:241
  421.5 11.8 %psum.56 = bf16[1,4608]{1,0:T(2,128)(2,1)S(1)} all-reduce(f32[1,4608]{1,0:T(1,128)S(1)} %convolution_dynamic-update-slice_fusion.1), channel_id=1, replica_groups=mesh['dp'=8,'tensor'=4] {'tensor'}, use_global_device_ids=true, to_apply=%region_25.26 | all-reduce | flops 4608 | bytes 27648 | tf_op jit(solution)/shard_map/psum | solution.py:361
  433.3 4.0 convolution_reduce_fusion.1
  439.7 6.0 broadcast_multiply_fusion
  446.7 13.3 %multiply_reduce_fusion = (f32[768]{0:T(1024)S(1)}, f32[768]{0:T(1024)S(1)}, f32[768]{0:T(1024)S(1)}, f32[768]{0:T(1024)S(1)}, f32[768]{0:T(1024)S(1)}, /*index=...) fusion(f32[1,32,32,768]{3,2,1,0:T(8,128)} %bitcast.206, f32[1024,768]{1,0:T(8,128)} %copy-done.11), kind=kLoop, calls=%fused_computation.141 | loop fusion | flops 12576768 | bytes 6316032 | tf_op jit(solution)/shard_map/reduce_sum | solution.py:58
  463.8 4.2 multiply_reduce_fusion.9
  468.2 40.3 %all-reduce.11 = (f32[4608]{0:T(1024)}, f32[9,768]{1,0:T(8,128)}, f32[768]{0:T(1024)}, f32[768]{0:T(1024)}, f32[9,768]{1,0:T(8,128)}, /*index=5*/f32[768]{0:T(1024)}) all-reduce(bf16[4608]{0:T(1024)(128)(2,1)S(1)} %convert_reduce_fusion.4, f32[9,768]{1,0:T(8,128)S(1)} %stack.85, ...), channel_id=1, replica_groups=mesh['dp'=8,'tensor'=4] {'dp'}, use_global_device_ids=true, to_apply=%region_28.29 | all-reduce | flops 20736 | bytes 156672 | tf_op jit(solution)/shard_map/psum | solution.py:381
  514.3 51.2 %reduce-scatter.32.cloned.1.call-done = f32[96,768]{1,0:T(8,128)} async-done(((f32[768,768]{1,0:T(8,128)}), f32[96,768]{1,0:T(8,128)}) %reduce-scatter.32.cloned.1.call-update) | async-done | bytes 294928 | tf_op jit(solution)/shard_map/reduce_scatter | solution.py:378
  565.5 65.3 %reduce-scatter.28.cloned.1.call-done = f32[96,192]{1,0:T(8,128)} async-done(((f32[768,192]{1,0:T(8,128)}), f32[96,192]{1,0:T(8,128)}) %reduce-scatter.28.cloned.1.call-update) | async-done | bytes 73744 | tf_op jit(solution)/shard_map/reduce_scatter | solution.py:376
  630.8 72.3 %reduce-scatter.26.cloned.1.call-done = f32[96,3,192]{2,0,1:T(8,128)} async-done(((f32[768,3,192]{2,0,1:T(8,128)}), f32[96,3,192]{2,0,1:T(8,128)}) %reduce-scatter.26.cloned.1.call-update) | async-done | bytes 221200 | tf_op jit(solution)/shard_map/reduce_scatter | solution.py:375
  703.1 131.2 %all-reduce.10.cloned.1.call-done = f32[1001,768]{1,0:T(8,128)} async-done(((f32[1001,768]{1,0:T(8,128)}), f32[1001,768]{1,0:T(8,128)}) %all-reduce.10.cloned.1.call-update) | async-done | bytes 3075088 | tf_op jit(solution)/shard_map/psum | solution.py:381
  834.2 233.0 %reduce-scatter.24.cloned.1.call-done = f32[576,768]{1,0:T(8,128)} async-done(((f32[4608,768]{1,0:T(8,128)}), f32[576,768]{1,0:T(8,128)}) %reduce-scatter.24.cloned.1.call-update) | async-done | bytes 1769488 | tf_op jit(solution)/shard_map/reduce_scatter | solution.py:379
  1067.3 3.7 copy.105
  (399 shorter events, 90.3 us)
Async XLA Ops:
  7.2 62.8 %reduce-scatter.12.cloned.1.call-start = ((), (), s32[]{:S(2)}) async-start(), calls=%async_computation.11 | async-start | bytes 1966080 | tf_op jit(solution)/shard_map/reduce_scatter | solution.py:221
  19.2 54.6 %copy-start.34 = (f32[768]{0:T(1024)}, f32[768]{0:T(1024)S(1)}, u32[]{:S(2)}) copy-start(f32[768]{0:T(1024)S(1)} %get-tuple-element.56) | copy-start | bytes 9220
  19.2 54.6 %copy-start.86 = (f32[768]{0:T(1024)}, f32[768]{0:T(1024)S(1)}, u32[]{:S(2)}) copy-start(f32[768]{0:T(1024)S(1)} %get-tuple-element.55) | copy-start | bytes 9220
  19.2 116.7 %copy-start.29 = (f32[768]{0:T(1024)}, f32[768]{0:T(1024)S(1)}, u32[]{:S(2)}) copy-start(f32[768]{0:T(1024)S(1)} %get-tuple-element.59) | copy-start | bytes 9220
  19.5 122.3 %copy-start.56 = (f32[768]{0:T(1024)}, f32[768]{0:T(1024)S(1)}, u32[]{:S(2)}) copy-start(f32[768]{0:T(1024)S(1)} %get-tuple-element.45) | copy-start | bytes 9220
  39.0 57.0 %all-gather.6.cloned.1.call-start = ((), (), s32[]{:S(2)}) async-start(), calls=%async_computation.12 | async-start | bytes 1966080 | tf_op jit(solution)/shard_map/all_gather | solution.py:233
  39.4 96.5 %copy-start.26 = (f32[768]{0:T(1024)}, f32[768]{0:T(1024)S(1)}, u32[]{:S(2)}) copy-start(f32[768]{0:T(1024)S(1)} %convert_element_type.211) | copy-start | bytes 9220
  39.4 96.5 %copy-start.31 = (f32[256]{0:T(256)}, f32[256]{0:T(256)S(1)}, u32[]{:S(2)}) copy-start(f32[256]{0:T(256)S(1)} %fusion.141) | copy-start | bytes 3076
  42.9 96.5 %copy-start.2 = (f32[1,1024,768]{2,1,0:T(8,128)}, f32[1,1024,768]{2,1,0:T(8,128)S(1)}, u32[]{:S(2)}) copy-start(f32[1,1024,768]{2,1,0:T(8,128)S(1)} %get-tuple-element.15) | copy-start | bytes 9437188
  42.9 33.4 %copy-start.113 = (bf16[768]{0:T(1024)(128)(2,1)S(1)}, bf16[768]{0:T(1024)(128)(2,1)}, u32[]{:S(2)}) copy-start(bf16[768]{0:T(1024)(128)(2,1)} %param.30) | copy-start | bytes 4612
  42.9 33.4 %copy-start.95 = (bf16[9,768]{1,0:T(8,128)(2,1)S(1)}, bf16[9,768]{1,0:T(8,128)(2,1)}, u32[]{:S(2)}) copy-start(bf16[9,768]{1,0:T(8,128)(2,1)} %param.31) | copy-start | bytes 41476
  76.2 59.7 %reduce-scatter.14.cloned.1.call-start = ((), (), s32[]{:S(2)}) async-start(), calls=%async_computation.13 | async-start | bytes 1966080 | tf_op jit(solution)/shard_map/reduce_scatter | solution.py:241
  105.0 30.9 %copy-start.18 = (bf16[256,768]{1,0:T(8,128)(2,1)S(1)}, bf16[256,768]{1,0:T(8,128)(2,1)}, u32[]{:S(2)}) copy-start(bf16[256,768]{1,0:T(8,128)(2,1)} %reduce-scatter.12.cloned.1.call-done) | copy-start | bytes 1179652
  107.6 88.1 %reduce-scatter.16.cloned.1.call-start = ((), (), s32[]{:S(2)}) async-start(), calls=%async_computation.15 | async-start | bytes 1966080 | tf_op jit(solution)/shard_map/reduce_scatter | solution.py:221
  161.4 34.3 %copy-start.27 = (f32[768]{0:T(1024)S(1)}, f32[768]{0:T(1024)}, u32[]{:S(2)}) copy-start(f32[768]{0:T(1024)} %copy-done.26) | copy-start | bytes 9220
  161.4 34.3 %copy-start.30 = (f32[768]{0:T(1024)S(1)}, f32[768]{0:T(1024)}, u32[]{:S(2)}) copy-start(f32[768]{0:T(1024)} %copy-done.29) | copy-start | bytes 9220
  161.4 34.3 %copy-start.32 = (f32[256]{0:T(256)S(1)}, f32[256]{0:T(256)}, u32[]{:S(2)}) copy-start(f32[256]{0:T(256)} %copy-done.31) | copy-start | bytes 3076
  164.6 33.5 %copy-start.35 = (f32[768]{0:T(1024)S(1)}, f32[768]{0:T(1024)}, u32[]{:S(2)}) copy-start(f32[768]{0:T(1024)} %copy-done.34) | copy-start | bytes 9220
  164.6 33.5 %copy-start.87 = (f32[768]{0:T(1024)S(1)}, f32[768]{0:T(1024)}, u32[]{:S(2)}) copy-start(f32[768]{0:T(1024)} %copy-done.86) | copy-start | bytes 9220
  167.4 51.6 %copy-start.110 = (f32[768]{0:T(1024)S(1)}, f32[768]{0:T(1024)}, u32[]{:S(2)}) copy-start(f32[768]{0:T(1024)} %copy-done.109) | copy-start | bytes 9220
  167.4 51.6 %all-gather.10.cloned.1.call-start = ((), (), s32[]{:S(2)}) async-start(), calls=%async_computation.16 | async-start | bytes 1966080 | tf_op jit(solution)/shard_map/all_gather | solution.py:233
  197.3 92.0 %copy-start.82 = (f32[256]{0:T(256)}, f32[256]{0:T(256)S(1)}, u32[]{:S(2)}) copy-start(f32[256]{0:T(256)S(1)} %broadcast_multiply_fusion.5) | copy-start | bytes 3076
  198.1 91.1 %copy-start.102 = (f32[256]{0:T(256)}, f32[256]{0:T(256)S(1)}, u32[]{:S(2)}) copy-start(f32[256]{0:T(256)S(1)} %fusion.135) | copy-start | bytes 3076
  199.2 41.0 %all-gather.8.cloned.1.call-start = ((), (), s32[]{:S(2)}) async-start(), calls=%async_computation.14 | async-start | bytes 1966080 | tf_op jit(solution)/shard_map/all_gather | solution.py:291
  199.8 24.1 %copy-start.39 = (f32[768]{0:T(1024)S(1)}, f32[768]{0:T(1024)}, u32[]{:S(2)}) copy-start(f32[768]{0:T(1024)} %copy-done.38) | copy-start | bytes 9220
  199.8 24.1 %copy-start.41 = (f32[768]{0:T(1024)S(1)}, f32[768]{0:T(1024)}, u32[]{:S(2)}) copy-start(f32[768]{0:T(1024)} %copy-done.40) | copy-start | bytes 9220
  199.8 24.1 %copy-start.43 = (f32[768]{0:T(1024)S(1)}, f32[768]{0:T(1024)}, u32[]{:S(2)}) copy-start(f32[768]{0:T(1024)} %copy-done.42) | copy-start | bytes 9220
  199.8 24.1 %copy-start.45 = (f32[768]{0:T(1024)S(1)}, f32[768]{0:T(1024)}, u32[]{:S(2)}) copy-start(f32[768]{0:T(1024)} %copy-done.44) | copy-start | bytes 9220
  199.9 87.7 %reduce-scatter.18.cloned.1.call-start = ((), (), s32[]{:S(2)}) async-start(), calls=%async_computation.17 | async-start | bytes 1966080 | tf_op jit(solution)/shard_map/reduce_scatter | solution.py:305
  259.2 32.6 %copy-start.92 = (f32[256]{0:T(256)S(1)}, f32[256]{0:T(256)}, u32[]{:S(2)}) copy-start(f32[256]{0:T(256)} %broadcast_select_fusion) | copy-start | bytes 3076
  259.3 54.4 %all-gather.12.cloned.1.call-start = ((), (), s32[]{:S(2)}) async-start(), calls=%async_computation.18 | async-start | bytes 1966080 | tf_op jit(solution)/shard_map/all_gather | solution.py:317
  290.9 30.8 %copy-start.100 = (f32[256]{0:T(256)}, f32[256]{0:T(256)S(1)}, u32[]{:S(2)}) copy-start(f32[256]{0:T(256)S(1)} %negate_multiply_fusion.1) | copy-start | bytes 3076
  293.8 73.9 %reduce-scatter.20.cloned.1.call-start = ((), (), s32[]{:S(2)}) async-start(), calls=%async_computation.19 | async-start | bytes 1966080 | tf_op jit(solution)/shard_map/reduce_scatter | solution.py:325
  335.0 32.8 %copy-start.116 = (bf16[768,768]{1,0:T(8,128)(2,1)S(1)}, bf16[768,768]{1,0:T(8,128)(2,1)}, u32[]{:S(2)}) copy-start(bf16[768,768]{1,0:T(8,128)(2,1)} %param.32) | copy-start | bytes 3538948
  335.0 32.8 %copy-start.119 = (bf16[1024,768]{1,0:T(8,128)(2,1)S(1)}, bf16[1024,768]{1,0:T(8,128)(2,1)}, u32[]{:S(2)}) copy-start(bf16[1024,768]{1,0:T(8,128)(2,1)} %get-tuple-element.80) | copy-start | bytes 4718596
  339.4 49.5 %all-gather.14.cloned.1.call-start = ((), (), s32[]{:S(2)}) async-start(), calls=%async_computation.20 | async-start | bytes 1966080 | tf_op jit(solution)/shard_map/all_gather | solution.py:333
  367.8 52.0 %reduce-scatter.22.cloned.1.call-start = ((), (), s32[]{:S(2)}) async-start(), calls=%async_computation.21 | async-start | bytes 1966080 | tf_op jit(solution)/shard_map/reduce_scatter | solution.py:241
  370.4 143.9 %reduce-scatter.30.cloned.1.call-start = ((), (), s32[]{:S(2)}) async-start(), calls=%async_computation.26 | async-start | bytes 2654208 | tf_op jit(solution)/shard_map/reduce_scatter | solution.py:377
  375.6 189.8 %reduce-scatter.32.cloned.1.call-start = ((), (), s32[]{:S(2)}) async-start(), calls=%async_computation.27 | async-start | bytes 2654208 | tf_op jit(solution)/shard_map/reduce_scatter | solution.py:378
  380.1 250.7 %reduce-scatter.28.cloned.1.call-start = ((), (), s32[]{:S(2)}) async-start(), calls=%async_computation.25 | async-start | bytes 884736 | tf_op jit(solution)/shard_map/reduce_scatter | solution.py:376
  383.1 319.9 %reduce-scatter.26.cloned.1.call-start = ((), (), s32[]{:S(2)}) async-start(), calls=%async_computation.24 | async-start | bytes 2654208 | tf_op jit(solution)/shard_map/reduce_scatter | solution.py:375
  388.0 446.3 %all-reduce.10.cloned.1.call-start = ((), (), s32[]{:S(2)}) async-start(), calls=%async_computation.22 | async-start | bytes 6193152 | tf_op jit(solution)/shard_map/psum | solution.py:381
  395.3 24.5 %copy-start.104 = (f32[768]{0:T(1024)S(1)}, f32[768]{0:T(1024)}, u32[]{:S(2)}) copy-start(f32[768]{0:T(1024)} %convert_element_type.218) | copy-start | bytes 9220
  439.4 627.9 %reduce-scatter.24.cloned.1.call-start = ((), (), s32[]{:S(2)}) async-start(), calls=%async_computation.23 | async-start | bytes 15925248 | tf_op jit(solution)/shard_map/reduce_scatter | solution.py:379
  463.8 44.7 %copy-start.33 = (f32[256]{0:T(256)S(1)}, f32[256]{0:T(256)}, u32[]{:S(2)}) copy-start(f32[256]{0:T(256)} %copy-done.31) | copy-start | bytes 3076
  463.8 44.7 %copy-start.37 = (f32[768]{0:T(1024)S(1)}, f32[768]{0:T(1024)}, u32[]{:S(2)}) copy-start(f32[768]{0:T(1024)} %copy-done.36) | copy-start | bytes 9220
  468.0 44.0 %copy-start.14 = (f32[256,768]{1,0:T(8,128)S(1)}, f32[256,768]{1,0:T(8,128)}, u32[]{:S(2)}) copy-start(f32[256,768]{1,0:T(8,128)} %copy-done.12) | copy-start | bytes 2359300
  512.0 559.0 %copy-start.1 = (bf16[1001,768]{1,0:T(8,128)(2,1)S(1)}, bf16[1001,768]{1,0:T(8,128)(2,1)}, u32[]{:S(2)}) copy-start(bf16[1001,768]{1,0:T(8,128)(2,1)} %param.22) | copy-start | bytes 4612612
  (89 other events, 657.7 us)
Sparse Core Ops, SparseCore 0:
  39.1 30.8 reduce-scatter.11
  76.3 19.6 all-gather.5
  107.7 28.1 reduce-scatter.13
  167.5 28.1 reduce-scatter.15
  199.3 19.6 all-gather.9
  220.5 19.6 all-gather.7
  259.4 28.1 reduce-scatter.17
  294.0 19.6 all-gather.11
  339.6 28.1 reduce-scatter.19
  369.2 19.6 all-gather.13
  391.6 28.1 reduce-scatter.21
  423.7 69.4 reduce-scatter.29
  497.3 68.1 reduce-scatter.31
  569.2 61.5 reduce-scatter.27
  635.1 67.8 reduce-scatter.25
  707.6 126.5 all-reduce.9
  838.8 228.4 reduce-scatter.23
where the time goes:
time: 1090 us; the launch traced here: 1080 us
  waiting for transfers between devices  779 us (71%)
  other arithmetic  99.6 us (9%)
  matrix products  75 us (7%)
  blocking collectives  52.1 us (5%)
  local copies, waits for them, and re-layouts  51.1 us (5%)
  between operations  18.2 us (2%)
    reduce_scatter x1, waiting for transfers between devices, shards(): lax.psum_scatter(grad_w_mod, 'dp', scatter_dimension=0, tiled=True)  233 us
    psum x1, waiting for transfers between devices, shards(): lax.psum((grad_k_att, grad_k_ffn, grad_b_up, grad_b_out, grad_b_down, gra...  131 us
    reduce_scatter x1, waiting for transfers between devices, shards(): lax.psum_scatter(grad_w_qkv, 'dp', scatter_dimension=0, tiled=True)  72.3 us
    reduce_scatter x1, waiting for transfers between devices, shards(): lax.psum_scatter(grad_w_out, 'dp', scatter_dimension=0, tiled=True)  65.3 us
    reduce_scatter x2, waiting for transfers between devices, forward_pass(): lax.psum_scatter(contract_last(attended, w_out).astype(jnp.bfloat16), 'te...  55.4 us
    reduce_scatter x1, waiting for transfers between devices, shards(): lax.psum_scatter(grad_w_down, 'dp', scatter_dimension=0, tiled=True)  51.2 us
    reduce_scatter x2, waiting for transfers between devices, forward_pass(): lax.psum_scatter(contract_last(activated, w_down).astype(jnp.bfloat16), '...  44.2 us
    psum x1, blocking collectives, shards(): lax.psum((grad_k_att, grad_k_ffn, grad_b_up, grad_b_out, grad_b_down, gra...  40.3 us
  transfers between devices with their start and end apart: 17, of which 16 were waited for; matrix products, arithmetic and copies ran while one was open for 8% of the time, Pallas kernels for 0%

commit v1 on v0

--- a/solution.py
+++ b/solution.py
@@ -9,6 +9,18 @@
 norm_eps = 1e-06
 score_scale = 0.125
 highest = lax.Precision.HIGHEST
+
+
+def collect(value, axis, dim):
+    ways, here, step = (lax.axis_size(axis), lax.axis_index(axis), value.shape[dim])
+    dims = [n * ways if d == dim else n for d, n in enumerate(value.shape)]
+    full = lax.dynamic_update_slice_in_dim(
+        jnp.zeros(dims, value.dtype), value, here * step, axis=dim
+    )
+    for far in range(1, ways):
+        value = lax.ppermute(value, axis, [(d, (d + 1) % ways) for d in range(ways)])
+        full = lax.dynamic_update_slice_in_dim(full, value, (here - far) % ways * step, axis=dim)
+    return full
 
 
 def layer_norm(values):
@@ -230,7 +242,7 @@
         middle = source_share + gate_att_rows * branch
         normed_ffn = layer_norm(middle)
         shaped_share = (normed_ffn * (1.0 + scale_ffn_rows) + shift_ffn_rows).astype(jnp.bfloat16)
-        shaped_ffn = lax.all_gather(shaped_share, "tensor", axis=0, tiled=True)
+        shaped_ffn = collect(shaped_share, "tensor", 0)
         hidden = jnp.dot(shaped_ffn, w_up, preferred_element_type=jnp.float32) + b_up.astype(
             jnp.float32
         )

time: 1090 us -> 1100 us (level)
  local copies, waits for them, and re-layouts: 51.1 us -> 64.1 us
    ppermute x0 -> x6, waiting for transfers between devices: none -> 42.3 us  [collect(): lax.ppermute(value, axis, [(d, (d + 1) % ways) for d in range(ways)])]
    all_gather x2 -> x0, waiting for transfers between devices: 38.4 us -> none  [forward_pass(): shaped_ffn = lax.all_gather(shaped_share, 'tensor', axis=0, tiled=True)]
  transfers between devices with their start and end apart: 17 -> 21, of which waited for: 16 -> 19; matrix products, arithmetic and copies ran while one was open for 8% -> 9% of each run, Pallas kernels for 0% -> 0%
where the time goes in v1:
time: 1100 us; the launch traced here: 1090 us
  waiting for transfers between devices  774 us (70%)
  other arithmetic  100 us (9%)
  matrix products  75 us (7%)
  local copies, waits for them, and re-layouts  64.1 us (6%)
  blocking collectives  52.1 us (5%)
  between operations  18.2 us (2%)
    reduce_scatter x1, waiting for transfers between devices, shards(): lax.psum_scatter(grad_w_mod, 'dp', scatter_dimension=0, tiled=True)  233 us
    psum x1, waiting for transfers between devices, shards(): lax.psum((grad_k_att, grad_k_ffn, grad_b_up, grad_b_out, grad_b_down, gra...  131 us
    reduce_scatter x1, waiting for transfers between devices, shards(): lax.psum_scatter(grad_w_qkv, 'dp', scatter_dimension=0, tiled=True)  72.4 us
    reduce_scatter x1, waiting for transfers between devices, shards(): lax.psum_scatter(grad_w_out, 'dp', scatter_dimension=0, tiled=True)  65.2 us
    reduce_scatter x2, waiting for transfers between devices, forward_pass(): lax.psum_scatter(contract_last(attended, w_out).astype(jnp.bfloat16), 'te...  55.4 us
    reduce_scatter x1, waiting for transfers between devices, shards(): lax.psum_scatter(grad_w_down, 'dp', scatter_dimension=0, tiled=True)  51.2 us
    reduce_scatter x2, waiting for transfers between devices, forward_pass(): lax.psum_scatter(contract_last(activated, w_down).astype(jnp.bfloat16), '...  46.1 us
    ppermute x6, waiting for transfers between devices, collect(): lax.ppermute(value, axis, [(d, (d + 1) % ways) for d in range(ways)])  42.3 us
  transfers between devices with their start and end apart: 21, of which 19 were waited for; matrix products, arithmetic and copies ran while one was open for 9% of the time, Pallas kernels for 0%

profile of v1, /device:TPU:0, one launch (start us, length us, event | category | flops | bytes accessed | tf_op | source)
XLA Modules:
  0.0 1086.3 jit_solution(9851774591386597575)
XLA Ops:
  13.5 5.1 convolution_reduce_fusion
  20.1 4.5 fusion.23
  27.6 5.4 reshape_reshape.15
  39.4 3.5 convert_bitcast_fusion
  42.9 27.1 %reduce-scatter.12.cloned.1.call-done = bf16[256,768]{1,0:T(8,128)(2,1)} async-done(((bf16[1024,768]{1,0:T(8,128)(2,1)}), bf16[256,768]{1,0:T(8,128)(2,1)}) %reduce-scatter.12.cloned.1.call-update) | async-done | bytes 393232 | tf_op jit(solution)/shard_map/reduce_scatter | solution.py:233
  77.4 7.2 collective-permute-done
  85.3 7.3 collective-permute-done.1
  101.9 3.2 convolution_add_fusion.1
  105.2 4.4 fusion.39
  115.3 27.2 %reduce-scatter.14.cloned.1.call-done = bf16[256,768]{1,0:T(8,128)(2,1)} async-done(((bf16[1024,768]{1,0:T(8,128)(2,1)}), bf16[256,768]{1,0:T(8,128)(2,1)}) %reduce-scatter.14.cloned.1.call-update) | async-done | bytes 393232 | tf_op jit(solution)/shard_map/reduce_scatter | solution.py:253
  148.5 4.5 add_convert_fusion
  155.9 5.4 reshape_reshape.16
  165.2 2.8 copy.57
  168.0 3.2 convert_element_type.230
  174.1 28.3 %reduce-scatter.16.cloned.1.call-done = bf16[256,768]{1,0:T(8,128)(2,1)} async-done(((bf16[1024,768]{1,0:T(8,128)(2,1)}), bf16[256,768]{1,0:T(8,128)(2,1)}) %reduce-scatter.16.cloned.1.call-update) | async-done | bytes 393232 | tf_op jit(solution)/shard_map/reduce_scatter | solution.py:233
  207.0 7.4 collective-permute-done.3
  214.5 15.2 %collective-permute-done.4 = bf16[256,768]{1,0:T(8,128)(2,1)S(1)} collective-permute-done((bf16[256,768]{1,0:T(8,128)(2,1)}, bf16[256,768]{1,0:T(8,128)(2,1)S(1)}, u32[]{:S(2)}, u32[]{:S(2)}) %collective-permute-start.4) | collective-permute-done | bytes 393248 | tf_op jit(solution)/shard_map/ppermute | solution.py:21
  232.4 4.6 collective-permute-done.5
  237.9 3.2 convolution_add_fusion
  242.8 5.7 multiply_add_fusion
  248.4 8.5 multiply_reduce_fusion.4
  258.7 5.1 convert_reduce_fusion.1
  267.6 28.2 %reduce-scatter.18.cloned.1.call-done = bf16[256,768]{1,0:T(8,128)(2,1)} async-done(((bf16[1024,768]{1,0:T(8,128)(2,1)}), bf16[256,768]{1,0:T(8,128)(2,1)}) %reduce-scatter.18.cloned.1.call-update) | async-done | bytes 393232 | tf_op jit(solution)/shard_map/reduce_scatter | solution.py:317
  302.3 19.6 %all-gather.6.cloned.1.call-done = bf16[1024,768]{1,0:T(8,128)(2,1)} async-done(((bf16[256,768]{1,0:T(8,128)(2,1)}), bf16[1024,768]{1,0:T(8,128)(2,1)}) %all-gather.6.cloned.1.call-update) | async-done | bytes 1572880 | tf_op jit(solution)/shard_map/all_gather | solution.py:329
  321.9 2.9 convolution_convert_fusion.6
  326.8 3.2 reshape_reshape.17
  336.6 3.2 copy.68
  339.9 3.4 reshape_reshape.18
  343.3 4.4 bitcast_convert_fusion
  347.7 28.3 %reduce-scatter.20.cloned.1.call-done = bf16[256,768]{1,0:T(8,128)(2,1)} async-done(((bf16[1024,768]{1,0:T(8,128)(2,1)}), bf16[256,768]{1,0:T(8,128)(2,1)}) %reduce-scatter.20.cloned.1.call-update) | async-done | bytes 393232 | tf_op jit(solution)/shard_map/reduce_scatter | solution.py:337
  379.2 4.7 fusion.156
  384.0 4.4 fusion.157
  388.5 2.9 fusion.155
  391.5 4.7 fusion.154
  399.3 4.4 fusion.72
  409.3 18.9 %reduce-scatter.22.cloned.1.call-done = bf16[256,768]{1,0:T(8,128)(2,1)} async-done(((bf16[1024,768]{1,0:T(8,128)(2,1)}), bf16[256,768]{1,0:T(8,128)(2,1)}) %reduce-scatter.22.cloned.1.call-update) | async-done | bytes 393232 | tf_op jit(solution)/shard_map/reduce_scatter | solution.py:253
  429.9 11.8 %psum.56 = bf16[1,4608]{1,0:T(2,128)(2,1)S(1)} all-reduce(f32[1,4608]{1,0:T(1,128)S(1)} %convolution_dynamic-update-slice_fusion.1), channel_id=1, replica_groups=mesh['dp'=8,'tensor'=4] {'tensor'}, use_global_device_ids=true, to_apply=%region_25.26 | all-reduce | flops 4608 | bytes 27648 | tf_op jit(solution)/shard_map/psum | solution.py:373
  441.7 4.0 convolution_reduce_fusion.1
  448.1 6.0 broadcast_multiply_fusion
  455.1 13.3 %multiply_reduce_fusion = (f32[768]{0:T(1024)S(1)}, f32[768]{0:T(1024)S(1)}, f32[768]{0:T(1024)S(1)}, f32[768]{0:T(1024)S(1)}, f32[768]{0:T(1024)S(1)}, /*index=...) fusion(f32[1,32,32,768]{3,2,1,0:T(8,128)} %bitcast.206, f32[1024,768]{1,0:T(8,128)} %copy-done.11), kind=kLoop, calls=%fused_computation.141 | loop fusion | flops 12576768 | bytes 6316032 | tf_op jit(solution)/shard_map/reduce_sum | solution.py:70
  472.2 4.2 multiply_reduce_fusion.9
  476.6 40.3 %all-reduce.11 = (f32[4608]{0:T(1024)}, f32[9,768]{1,0:T(8,128)}, f32[768]{0:T(1024)}, f32[768]{0:T(1024)}, f32[9,768]{1,0:T(8,128)}, /*index=5*/f32[768]{0:T(1024)}) all-reduce(bf16[4608]{0:T(1024)(128)(2,1)S(1)} %convert_reduce_fusion.4, f32[9,768]{1,0:T(8,128)S(1)} %stack.85, ...), channel_id=1, replica_groups=mesh['dp'=8,'tensor'=4] {'dp'}, use_global_device_ids=true, to_apply=%region_28.29 | all-reduce | flops 20736 | bytes 156672 | tf_op jit(solution)/shard_map/psum | solution.py:393
  522.8 51.2 %reduce-scatter.32.cloned.1.call-done = f32[96,768]{1,0:T(8,128)} async-done(((f32[768,768]{1,0:T(8,128)}), f32[96,768]{1,0:T(8,128)}) %reduce-scatter.32.cloned.1.call-update) | async-done | bytes 294928 | tf_op jit(solution)/shard_map/reduce_scatter | solution.py:390
  574.0 65.2 %reduce-scatter.28.cloned.1.call-done = f32[96,192]{1,0:T(8,128)} async-done(((f32[768,192]{1,0:T(8,128)}), f32[96,192]{1,0:T(8,128)}) %reduce-scatter.28.cloned.1.call-update) | async-done | bytes 73744 | tf_op jit(solution)/shard_map/reduce_scatter | solution.py:388
  639.2 72.4 %reduce-scatter.26.cloned.1.call-done = f32[96,3,192]{2,0,1:T(8,128)} async-done(((f32[768,3,192]{2,0,1:T(8,128)}), f32[96,3,192]{2,0,1:T(8,128)}) %reduce-scatter.26.cloned.1.call-update) | async-done | bytes 221200 | tf_op jit(solution)/shard_map/reduce_scatter | solution.py:387
  711.6 131.2 %all-reduce.10.cloned.1.call-done = f32[1001,768]{1,0:T(8,128)} async-done(((f32[1001,768]{1,0:T(8,128)}), f32[1001,768]{1,0:T(8,128)}) %all-reduce.10.cloned.1.call-update) | async-done | bytes 3075088 | tf_op jit(solution)/shard_map/psum | solution.py:393
  842.9 233.0 %reduce-scatter.24.cloned.1.call-done = f32[576,768]{1,0:T(8,128)} async-done(((f32[4608,768]{1,0:T(8,128)}), f32[576,768]{1,0:T(8,128)}) %reduce-scatter.24.cloned.1.call-update) | async-done | bytes 1769488 | tf_op jit(solution)/shard_map/reduce_scatter | solution.py:391
  1075.9 3.7 copy.113
  (419 shorter events, 109.5 us)
Async XLA Ops:
  7.2 62.8 %reduce-scatter.12.cloned.1.call-start = ((), (), s32[]{:S(2)}) async-start(), calls=%async_computation.11 | async-start | bytes 1966080 | tf_op jit(solution)/shard_map/reduce_scatter | solution.py:233
  19.2 55.8 %copy-start.36 = (f32[768]{0:T(1024)}, f32[768]{0:T(1024)S(1)}, u32[]{:S(2)}) copy-start(f32[768]{0:T(1024)S(1)} %get-tuple-element.56) | copy-start | bytes 9220
  19.2 123.3 %copy-start.31 = (f32[768]{0:T(1024)}, f32[768]{0:T(1024)S(1)}, u32[]{:S(2)}) copy-start(f32[768]{0:T(1024)S(1)} %get-tuple-element.59) | copy-start | bytes 9220
  39.0 103.5 %reduce-scatter.14.cloned.1.call-start = ((), (), s32[]{:S(2)}) async-start(), calls=%async_computation.12 | async-start | bytes 1966080 | tf_op jit(solution)/shard_map/reduce_scatter | solution.py:253
  39.4 103.1 %copy-start.28 = (f32[768]{0:T(1024)}, f32[768]{0:T(1024)S(1)}, u32[]{:S(2)}) copy-start(f32[768]{0:T(1024)S(1)} %convert_element_type.211) | copy-start | bytes 9220
  39.4 103.1 %copy-start.33 = (f32[256]{0:T(256)}, f32[256]{0:T(256)S(1)}, u32[]{:S(2)}) copy-start(f32[256]{0:T(256)S(1)} %fusion.141) | copy-start | bytes 3076
  42.9 103.1 %copy-start.2 = (f32[1,1024,768]{2,1,0:T(8,128)}, f32[1,1024,768]{2,1,0:T(8,128)S(1)}, u32[]{:S(2)}) copy-start(f32[1,1024,768]{2,1,0:T(8,128)S(1)} %get-tuple-element.15) | copy-start | bytes 9437188
  77.4 7.2 collective-permute-start
  85.3 7.3 collective-permute-start.1
  92.6 7.5 collective-permute-start.2
  93.3 11.8 %copy-start.112 = (f32[768]{0:T(1024)}, f32[768]{0:T(1024)S(1)}, u32[]{:S(2)}) copy-start(f32[768]{0:T(1024)S(1)} %convert_element_type.214) | copy-start | bytes 9220
  96.0 9.1 copy-start.40
  96.0 9.1 copy-start.42
  113.5 88.9 %reduce-scatter.16.cloned.1.call-start = ((), (), s32[]{:S(2)}) async-start(), calls=%async_computation.14 | async-start | bytes 1966080 | tf_op jit(solution)/shard_map/reduce_scatter | solution.py:233
  115.3 30.7 %copy-start.95 = (f32[256]{0:T(256)}, f32[256]{0:T(256)S(1)}, u32[]{:S(2)}) copy-start(f32[256]{0:T(256)S(1)} %broadcast_select_fusion) | copy-start | bytes 3076
  168.0 34.3 %copy-start.29 = (f32[768]{0:T(1024)S(1)}, f32[768]{0:T(1024)}, u32[]{:S(2)}) copy-start(f32[768]{0:T(1024)} %copy-done.28) | copy-start | bytes 9220
  168.0 34.3 %copy-start.32 = (f32[768]{0:T(1024)S(1)}, f32[768]{0:T(1024)}, u32[]{:S(2)}) copy-start(f32[768]{0:T(1024)} %copy-done.31) | copy-start | bytes 9220
  168.0 34.3 %copy-start.34 = (f32[256]{0:T(256)S(1)}, f32[256]{0:T(256)}, u32[]{:S(2)}) copy-start(f32[256]{0:T(256)} %copy-done.33) | copy-start | bytes 3076
  174.0 30.8 %copy-start.37 = (f32[768]{0:T(1024)S(1)}, f32[768]{0:T(1024)}, u32[]{:S(2)}) copy-start(f32[768]{0:T(1024)} %copy-done.36) | copy-start | bytes 9220
  174.0 30.8 %copy-start.90 = (f32[768]{0:T(1024)S(1)}, f32[768]{0:T(1024)}, u32[]{:S(2)}) copy-start(f32[768]{0:T(1024)} %get-tuple-element.55) | copy-start | bytes 9220
  174.0 74.4 %all-gather.4.cloned.1.call-start = ((), (), s32[]{:S(2)}) async-start(), calls=%async_computation.13 | async-start | bytes 1966080 | tf_op jit(solution)/shard_map/all_gather | solution.py:303
  203.9 93.5 %copy-start.85 = (f32[256]{0:T(256)}, f32[256]{0:T(256)S(1)}, u32[]{:S(2)}) copy-start(f32[256]{0:T(256)S(1)} %broadcast_multiply_fusion.5) | copy-start | bytes 3076
  204.2 33.6 %copy-start.113 = (f32[768]{0:T(1024)S(1)}, f32[768]{0:T(1024)}, u32[]{:S(2)}) copy-start(f32[768]{0:T(1024)} %copy-done.112) | copy-start | bytes 9220
  204.2 93.3 %copy-start.103 = (f32[256]{0:T(256)}, f32[256]{0:T(256)S(1)}, u32[]{:S(2)}) copy-start(f32[256]{0:T(256)S(1)} %fusion.135) | copy-start | bytes 3076
  207.0 7.5 collective-permute-start.3
  207.0 88.8 %reduce-scatter.18.cloned.1.call-start = ((), (), s32[]{:S(2)}) async-start(), calls=%async_computation.15 | async-start | bytes 1966080 | tf_op jit(solution)/shard_map/reduce_scatter | solution.py:317
  214.5 15.2 %collective-permute-start.4 = (bf16[256,768]{1,0:T(8,128)(2,1)}, bf16[256,768]{1,0:T(8,128)(2,1)S(1)}, u32[]{:S(2)}, u32[]{:S(2)}) collective-permute-start(bf16[256,768]{1,0:T(8,128)(2,1)} %collective-permute-done.3), channel_id=1, source_target_pairs={{0,1},{1,2},{2,3},{3,0},{4,5},{5,6},{6,7},{7,4},{8,9},{9,10},{10,1... | collective-permute-start | bytes 1179656 | tf_op jit(solution)/shard_map/ppermute | solution.py:21
  229.7 7.4 collective-permute-start.5
  267.5 32.5 %copy-start.96 = (f32[256]{0:T(256)S(1)}, f32[256]{0:T(256)}, u32[]{:S(2)}) copy-start(f32[256]{0:T(256)} %copy-done.95) | copy-start | bytes 3076
  267.5 54.4 %all-gather.6.cloned.1.call-start = ((), (), s32[]{:S(2)}) async-start(), calls=%async_computation.16 | async-start | bytes 1966080 | tf_op jit(solution)/shard_map/all_gather | solution.py:329
  299.1 30.9 %copy-start.105 = (f32[256]{0:T(256)}, f32[256]{0:T(256)S(1)}, u32[]{:S(2)}) copy-start(f32[256]{0:T(256)S(1)} %negate_multiply_fusion.1) | copy-start | bytes 3076
  302.1 74.0 %reduce-scatter.20.cloned.1.call-start = ((), (), s32[]{:S(2)}) async-start(), calls=%async_computation.17 | async-start | bytes 1966080 | tf_op jit(solution)/shard_map/reduce_scatter | solution.py:337
  343.3 32.8 %copy-start.119 = (bf16[768,768]{1,0:T(8,128)(2,1)S(1)}, bf16[768,768]{1,0:T(8,128)(2,1)}, u32[]{:S(2)}) copy-start(bf16[768,768]{1,0:T(8,128)(2,1)} %param.32) | copy-start | bytes 3538948
  343.3 32.8 %copy-start.122 = (bf16[1024,768]{1,0:T(8,128)(2,1)S(1)}, bf16[1024,768]{1,0:T(8,128)(2,1)}, u32[]{:S(2)}) copy-start(bf16[1024,768]{1,0:T(8,128)(2,1)} %get-tuple-element.84) | copy-start | bytes 4718596
  347.7 49.7 %all-gather.8.cloned.1.call-start = ((), (), s32[]{:S(2)}) async-start(), calls=%async_computation.18 | async-start | bytes 1966080 | tf_op jit(solution)/shard_map/all_gather | solution.py:345
  376.1 52.2 %reduce-scatter.22.cloned.1.call-start = ((), (), s32[]{:S(2)}) async-start(), calls=%async_computation.19 | async-start | bytes 1966080 | tf_op jit(solution)/shard_map/reduce_scatter | solution.py:253
  378.7 144.1 %reduce-scatter.30.cloned.1.call-start = ((), (), s32[]{:S(2)}) async-start(), calls=%async_computation.24 | async-start | bytes 2654208 | tf_op jit(solution)/shard_map/reduce_scatter | solution.py:389
  384.0 190.0 %reduce-scatter.32.cloned.1.call-start = ((), (), s32[]{:S(2)}) async-start(), calls=%async_computation.25 | async-start | bytes 2654208 | tf_op jit(solution)/shard_map/reduce_scatter | solution.py:390
  388.5 250.7 %reduce-scatter.28.cloned.1.call-start = ((), (), s32[]{:S(2)}) async-start(), calls=%async_computation.23 | async-start | bytes 884736 | tf_op jit(solution)/shard_map/reduce_scatter | solution.py:388
  391.4 320.2 %reduce-scatter.26.cloned.1.call-start = ((), (), s32[]{:S(2)}) async-start(), calls=%async_computation.22 | async-start | bytes 2654208 | tf_op jit(solution)/shard_map/reduce_scatter | solution.py:387
  396.3 446.6 %all-reduce.10.cloned.1.call-start = ((), (), s32[]{:S(2)}) async-start(), calls=%async_computation.20 | async-start | bytes 6193152 | tf_op jit(solution)/shard_map/psum | solution.py:393
  403.7 24.5 %copy-start.107 = (f32[768]{0:T(1024)S(1)}, f32[768]{0:T(1024)}, u32[]{:S(2)}) copy-start(f32[768]{0:T(1024)} %convert_element_type.218) | copy-start | bytes 9220
  447.8 628.1 %reduce-scatter.24.cloned.1.call-start = ((), (), s32[]{:S(2)}) async-start(), calls=%async_computation.21 | async-start | bytes 15925248 | tf_op jit(solution)/shard_map/reduce_scatter | solution.py:391
  455.1 15.3 %copy-start.4 = (f32[1,1024,768]{2,1,0:T(8,128)S(1)}, f32[1,1024,768]{2,1,0:T(8,128)}, u32[]{:S(2)}) copy-start(f32[1,1024,768]{2,1,0:T(8,128)} %copy-done.3) | copy-start | bytes 9437188
  472.2 44.8 %copy-start.35 = (f32[256]{0:T(256)S(1)}, f32[256]{0:T(256)}, u32[]{:S(2)}) copy-start(f32[256]{0:T(256)} %copy-done.33) | copy-start | bytes 3076
  472.2 44.8 %copy-start.39 = (f32[768]{0:T(1024)S(1)}, f32[768]{0:T(1024)}, u32[]{:S(2)}) copy-start(f32[768]{0:T(1024)} %copy-done.38) | copy-start | bytes 9220
  476.4 44.1 %copy-start.14 = (f32[256,768]{1,0:T(8,128)S(1)}, f32[256,768]{1,0:T(8,128)}, u32[]{:S(2)}) copy-start(f32[256,768]{1,0:T(8,128)} %copy-done.12) | copy-start | bytes 2359300
  520.6 559.1 %copy-start.1 = (bf16[1001,768]{1,0:T(8,128)(2,1)S(1)}, bf16[1001,768]{1,0:T(8,128)(2,1)}, u32[]{:S(2)}) copy-start(bf16[1001,768]{1,0:T(8,128)(2,1)} %param.22) | copy-start | bytes 4612612
  (96 other events, 407.5 us)
Sparse Core Ops, SparseCore 0:
  39.1 30.8 reduce-scatter.11
  113.6 28.8 reduce-scatter.13
  174.1 28.1 reduce-scatter.15
  207.1 24.6 all-gather.3
  267.7 28.1 reduce-scatter.17
  302.2 19.6 all-gather.5
  347.8 28.1 reduce-scatter.19
  377.7 19.6 all-gather.7
  400.1 28.1 reduce-scatter.21
  432.2 69.4 reduce-scatter.29
  505.8 68.1 reduce-scatter.31
  577.7 61.4 reduce-scatter.27
  643.6 67.9 reduce-scatter.25
  716.2 126.6 all-reduce.9
  847.4 228.4 reduce-scatter.23
